TPU v7x, 32 devices: a whole 2x2x4 slice. The times are simulated.
32 devices in a mesh: expert: 8 (over z, x), tensor: 4 (over y, core).
Axes of the slice: x: 2, y: 2, z: 4, core: 2. Of those that a mesh axis runs over, the one named last changes fastest.
Arguments:
- tokens: bfloat16 [512, 8192], P('expert', 'tensor'), may hold values from -6 to 6
- frozen_gate_weight: bfloat16 [8192, 28672], P('tensor', 'expert'), may hold values from -0.0625 to 0.0625
- frozen_up_weight: bfloat16 [8192, 28672], P('tensor', 'expert'), may hold values from -0.0625 to 0.0625
- frozen_down_weight: bfloat16 [28672, 8192], P('expert', 'tensor'), may hold values from -0.03125 to 0.03125
- adapter_down_weight: bfloat16 [32, 8192, 128], P('expert', 'tensor'), may hold values from -0.0625 to 0.0625
- adapter_up_weight: bfloat16 [32, 128, 8192], P('expert', None, 'tensor'), may hold values from -0.0625 to 0.0625
- routes: int32 [512, 2], P('expert'), may hold values from 0 to 31, all different within a row; in each aligned block of 64 rows (0 to 63, 64 to 127, ...) at most 8 rows name the same one
- route_gate_weights: float32 [512, 2], P('expert'), may hold values from 0.1 to 1
- output_gradient: bfloat16 [512, 8192], P('expert', 'tensor'), may hold values from -6 to 6
Outputs:
- ffn_out: bfloat16 [512, 8192], P('expert', 'tensor')
- grad_down: bfloat16 [32, 8192, 128], P('expert', 'tensor')
- grad_up: bfloat16 [32, 128, 8192], P('expert', None, 'tensor')
Inputs may be any that keep to these rules, and one draw needn't show every extreme that they name: `routes`: the two experts of a token differ. Among the 64 rows of one index of expert no expert is named more than 8 times, and in some such rows one expert is named exactly 8 times.
All inputs are finite; a program needn't handle non-finite values.
Results may differ from a plain program's by a relative error of at most 0.025.
Values may be sent and summed in bfloat16 or wider, within the bound.
A program may use at most 128 MiB of HBM per device.

v0:
```python
import jax
import jax.numpy as jnp
from jax import lax
from jax.sharding import PartitionSpec as P


def activate(summed, hidden_width):
    gate_part = summed[:, :hidden_width]
    up_part = summed[:, hidden_width:]
    return (jax.nn.silu(gate_part) * up_part).astype(jnp.bfloat16)


def per_device(
    tokens,
    frozen_gate_weight,
    frozen_up_weight,
    frozen_down_weight,
    adapter_down_weight,
    adapter_up_weight,
    routes,
    route_gate_weights,
    output_gradient,
):
    n_expert = lax.axis_size("expert")
    tok_count, width_part = tokens.shape
    hidden_width = frozen_gate_weight.shape[1]
    expert_resident = adapter_down_weight.shape[0]
    all_experts = expert_resident * n_expert
    most_slots = max(2, 4 * tok_count // all_experts)
    slot_total = all_experts * most_slots
    per_peer = expert_resident * most_slots
    shard_rows = lax.all_gather(tokens, "expert", axis=0, tiled=True)
    gate_part = jnp.dot(shard_rows, frozen_gate_weight, preferred_element_type=jnp.float32)
    up_part = jnp.dot(shard_rows, frozen_up_weight, preferred_element_type=jnp.float32)
    partial_value = jnp.concatenate([gate_part, up_part], axis=1)
    summed = lax.psum_scatter(
        partial_value.astype(jnp.bfloat16), "tensor", scatter_dimension=0, tiled=True
    ).astype(jnp.float32)
    hidden_all = lax.all_gather(activate(summed, hidden_width), "tensor", axis=0, tiled=True)
    base_out = lax.psum_scatter(
        jnp.dot(hidden_all, frozen_down_weight, preferred_element_type=jnp.float32).astype(
            jnp.bfloat16
        ),
        "expert",
        scatter_dimension=0,
        tiled=True,
    ).astype(jnp.float32)
    route_ids = routes.reshape(-1)
    pair_count = route_ids.shape[0]
    expert_range = jnp.arange(all_experts, dtype=jnp.int32)
    member = (route_ids[:, None] == expert_range[None, :]).astype(jnp.bfloat16)
    pair_range = jnp.arange(pair_count, dtype=jnp.int32)
    before = (pair_range[:, None] > pair_range[None, :]).astype(jnp.bfloat16)
    earlier = jnp.dot(before, member, preferred_element_type=jnp.float32)
    within = jnp.sum(earlier * member.astype(jnp.float32), axis=1).astype(jnp.int32)
    target = route_ids * most_slots + within
    slot_range = jnp.arange(slot_total, dtype=jnp.int32)
    select = (slot_range[:, None] == target[None, :]).astype(jnp.bfloat16)
    to_slots = jnp.sum(select.reshape(slot_total, tok_count, 2), axis=2)
    send_inputs = jnp.dot(to_slots, tokens, preferred_element_type=jnp.float32).astype(jnp.bfloat16)
    send_inputs = send_inputs.reshape(n_expert, per_peer, width_part)
    scaled = (
        route_gate_weights[:, :, None] * output_gradient[:, None, :].astype(jnp.float32)
    ).astype(jnp.bfloat16)
    scaled = scaled.reshape(pair_count, width_part)
    send_grads = jnp.dot(select, scaled, preferred_element_type=jnp.float32).astype(jnp.bfloat16)
    send_grads = send_grads.reshape(n_expert, per_peer, width_part)
    incoming_input_rows = lax.all_to_all(
        send_inputs, "expert", split_axis=0, concat_axis=0, tiled=True
    )
    incoming_input_rows = incoming_input_rows.reshape(
        n_expert, expert_resident, most_slots, width_part
    )
    low_sum = lax.psum(
        jnp.einsum(
            "bcwk,cko->cbwo",
            incoming_input_rows,
            adapter_down_weight,
            preferred_element_type=jnp.float32,
        ).astype(jnp.bfloat16),
        "tensor",
    )
    expert_out = jnp.einsum(
        "lugx,lxo->ulgo", low_sum, adapter_up_weight, preferred_element_type=jnp.float32
    ).astype(jnp.bfloat16)
    returned = lax.all_to_all(
        expert_out.reshape(n_expert, per_peer, width_part),
        "expert",
        split_axis=0,
        concat_axis=0,
        tiled=True,
    )
    per_pair = jnp.dot(
        select.T, returned.reshape(slot_total, width_part), preferred_element_type=jnp.float32
    )
    per_pair = per_pair.reshape(tok_count, 2, width_part)
    adapter_sum = (
        route_gate_weights[:, 0:1] * per_pair[:, 0, :]
        + route_gate_weights[:, 1:2] * per_pair[:, 1, :]
    )
    ffn_out = (base_out + adapter_sum).astype(jnp.bfloat16)
    incoming_gradients = lax.all_to_all(
        send_grads, "expert", split_axis=0, concat_axis=0, tiled=True
    )
    incoming_gradients = incoming_gradients.reshape(
        n_expert, expert_resident, most_slots, width_part
    )
    back_sum = lax.psum(
        jnp.einsum(
            "nhpf,hxf->hnpx",
            incoming_gradients,
            adapter_up_weight,
            preferred_element_type=jnp.float32,
        ).astype(jnp.bfloat16),
        "tensor",
    )
    grad_up = jnp.einsum(
        "jsmr,sjmd->jrd", low_sum, incoming_gradients, preferred_element_type=jnp.float32
    ).astype(jnp.bfloat16)
    grad_down = jnp.einsum(
        "sjmd,jsmr->jdr", incoming_input_rows, back_sum, preferred_element_type=jnp.float32
    ).astype(jnp.bfloat16)
    return (ffn_out, grad_down, grad_up)


def solution(mesh):
    placed = (
        P("expert", "tensor"),
        P("tensor", "expert"),
        P("tensor", "expert"),
        P("expert", "tensor"),
        P("expert", "tensor", None),
        P("expert", None, "tensor"),
        P("expert", None),
        P("expert", None),
        P("expert", "tensor"),
    )
    return jax.shard_map(
        per_device,
        mesh=mesh,
        in_specs=placed,
        out_specs=(P("expert", "tensor"), P("expert", "tensor", None), P("expert", None, "tensor")),
        check_vma=False,
    )
```

profile of v0, /device:TPU:0, one launch (start us, length us, event | category | flops | bytes accessed | tf_op | source)
XLA Modules:
  0.0 356.5 jit_solution(9830163328550035932)
XLA Ops:
  7.2 0.0 all-gather.3.cloned.1.call-start
  7.2 0.7 all-gather.3.cloned.1.call-update
  7.9 0.0 reduce-scatter.3.cloned.1.call-start
  8.0 54.0 %all-gather.3.cloned.1.call-done = bf16[512,2048]{1,0:T(8,128)(2,1)} async-done(((bf16[64,2048]{1,0:T(8,128)(2,1)}), bf16[512,2048]{1,0:T(8,128)(2,1)}) %all-gather.3.cloned.1.call-update) | async-done | bytes 2097168 | tf_op jit(solution)/shard_map/all_gather | solution.py:32
  62.0 14.9 %convolution_convert_fusion = bf16[512,3584]{1,0:T(8,128)(2,1)} fusion(bf16[512,2048]{1,0:T(8,128)(2,1)} %all-gather.3.cloned.1.call-done, bf16[2048,3584]{1,0:T(8,128)(2,1)} %param.11), kind=kOutput, calls=%fused_computation.1 | convolution fusion | flops 7518027776 | bytes 20447232 | tf_op jit(solution)/shard_map/dot_general | solution.py:34
  76.9 12.4 %convolution_convert_fusion.1 = bf16[512,3584]{1,0:T(8,128)(2,1)} fusion(bf16[512,2048]{1,0:T(8,128)(2,1)S(1)} %copy-done.6, bf16[2048,3584]{1,0:T(8,128)(2,1)} %param.10), kind=kOutput, calls=%fused_computation.2 | convolution fusion | flops 7518027776 | bytes 20447232 | tf_op jit(solution)/shard_map/dot_general | solution.py:33
  89.3 6.9 %pad_maximum_fusion = bf16[512,7168]{1,0:T(8,128)(2,1)} fusion(bf16[512,3584]{1,0:T(8,128)(2,1)} %convolution_convert_fusion, bf16[512,3584]{1,0:T(8,128)(2,1)} %convolution_convert_fusion.1), kind=kLoop, calls=%fused_computation | loop fusion | flops 14680064 | bytes 14680064 | tf_op jit(solution)/shard_map/concatenate | solution.py:35
  96.1 0.0 reduce-scatter.3.cloned.1.call-update
  96.2 0.0 all-gather.5.cloned.1.call-start
  96.2 64.6 %reduce-scatter.3.cloned.1.call-done = bf16[128,7168]{1,0:T(8,128)(2,1)} async-done(((bf16[512,7168]{1,0:T(8,128)(2,1)}), bf16[128,7168]{1,0:T(8,128)(2,1)}) %reduce-scatter.3.cloned.1.call-update) | async-done | bytes 1835024 | tf_op jit(solution)/shard_map/reduce_scatter | solution.py:36
  160.8 1.9 convert_element_type.72
  162.7 1.5 fusion.6
  164.1 0.0 all-gather.5.cloned.1.call-update
  164.2 0.1 copy.40
  164.3 0.1 reshape.81
  164.4 0.5 mul.78
  164.9 1.7 mul.79
  166.6 0.1 copy.45
  166.7 0.1 mul.76
  166.9 0.2 fusion.13
  167.1 2.7 convolution_convert_fusion.3
  169.8 5.5 %all-to-all-start.2 = ((bf16[8,32,2048]{2,1,0:T(8,128)(2,1)}), bf16[8,32,2048]{2,1,0:T(8,128)(2,1)S(1)}, u32[]{:S(2)}, u32[]{:S(2)}) async-start(bf16[8,32,2048]{2,1,0:T(8,128)(2,1)} %bitcast.77), calls=%async_computation.4 | async-start | bytes 2097152 | tf_op jit(solution)/shard_map/all_to_all | solution.py:102
  175.3 0.1 convert_element_type.79
  175.5 0.1 copy.41
  175.5 0.1 fusion.25
  175.7 1.4 convolution_convert_fusion.5
  177.1 23.9 %all-to-all-done.2 = bf16[8,32,2048]{2,1,0:T(8,128)(2,1)S(1)} async-done(((bf16[8,32,2048]{2,1,0:T(8,128)(2,1)}), bf16[8,32,2048]{2,1,0:T(8,128)(2,1)S(1)}, u32[]{:S(2)}, u32[]{:S(2)}) %all-to-all-start.2) | async-done | bytes 1048608 | tf_op jit(solution)/shard_map/all_to_all | solution.py:102
  201.0 4.3 %all-to-all-start = ((bf16[8,32,2048]{2,1,0:T(8,128)(2,1)}), bf16[8,32,2048]{2,1,0:T(8,128)(2,1)}, u32[]{:S(2)}, u32[]{:S(2)}) async-start(bf16[8,32,2048]{2,1,0:T(8,128)(2,1)} %bitcast.76), calls=%async_computation.2 | async-start | bytes 2097152 | tf_op jit(solution)/shard_map/all_to_all | solution.py:68
  205.2 0.0 all-reduce.3.cloned.1.call-start
  205.3 0.6 copy.46
  205.9 1.5 fusion.7
  207.4 23.4 %all-to-all-done = bf16[8,32,2048]{2,1,0:T(8,128)(2,1)} async-done(((bf16[8,32,2048]{2,1,0:T(8,128)(2,1)}), bf16[8,32,2048]{2,1,0:T(8,128)(2,1)}, u32[]{:S(2)}, u32[]{:S(2)}) %all-to-all-start) | async-done | bytes 1048608 | tf_op jit(solution)/shard_map/all_to_all | solution.py:68
  230.8 3.0 fusion.10
  233.8 0.0 all-reduce.3.cloned.1.call-update
  233.8 0.2 reduce-scatter.5.cloned.1.call-start
  234.0 0.0 all-gather.5.cloned.1.call-done
  234.1 13.1 %convolution_convert_fusion.2 = bf16[512,2048]{1,0:T(8,128)(2,1)} fusion(bf16[512,3584]{1,0:T(8,128)(2,1)} %all-gather.5.cloned.1.call-done, bf16[3584,2048]{1,0:T(8,128)(2,1)} %param.12), kind=kOutput, calls=%fused_computation.5 | convolution fusion | flops 7517241344 | bytes 20447232 | tf_op jit(solution)/shard_map/dot_general | solution.py:41
  247.2 16.4 %all-reduce.3.cloned.1.call-done = (bf16[4,8,8,128]{3,2,1,0:T(8,128)(2,1)}, bf16[4,8,8,128]{3,1,2,0:T(8,128)(2,1)}) async-done(((bf16[4,8,8,128]{3,2,1,0:T(8,128)(2,1)}, bf16[4,8,8,128]{3,1,2,0:T(8,128)(2,1)}), (bf16[4,8,8,128]{3,2,1,0:T(8,128)(2,1)}, bf16[4,8,8,128]{3,1,2,0:T(8,128)(2,1)})) %all-reduce.3.cloned.1.call-update) | async-done | bytes 131088 | tf_op jit(solution)/shard_map/psum | solution.py:74
  263.6 1.3 fusion
  264.9 1.1 copy.62
  266.0 5.5 %all-to-all-start.1 = ((bf16[8,32,2048]{2,1,0:T(8,128)(2,1)}), bf16[8,32,2048]{2,1,0:T(8,128)(2,1)}, u32[]{:S(2)}, u32[]{:S(2)}) async-start(bf16[8,32,2048]{2,1,0:T(8,128)(2,1)} %bitcast.75), calls=%async_computation.3 | async-start | bytes 2097152 | tf_op jit(solution)/shard_map/all_to_all | solution.py:86
  271.5 0.1 iota_compare_fusion.2
  271.7 2.1 bitcast_convert_fusion
  273.7 3.5 bitcast_convert_fusion.1
  277.2 36.2 %all-to-all-done.1 = bf16[8,32,2048]{2,1,0:T(8,128)(2,1)} async-done(((bf16[8,32,2048]{2,1,0:T(8,128)(2,1)}), bf16[8,32,2048]{2,1,0:T(8,128)(2,1)}, u32[]{:S(2)}, u32[]{:S(2)}) %all-to-all-start.1) | async-done | bytes 1048608 | tf_op jit(solution)/shard_map/all_to_all | solution.py:86
  313.4 1.5 fusion.23
  314.9 33.2 %reduce-scatter.5.cloned.1.call-done = bf16[64,2048]{1,0:T(8,128)(2,1)} async-done(((bf16[512,2048]{1,0:T(8,128)(2,1)}), bf16[64,2048]{1,0:T(8,128)(2,1)}) %reduce-scatter.5.cloned.1.call-update) | async-done | bytes 262160 | tf_op jit(solution)/shard_map/reduce_scatter | solution.py:40
  348.2 1.8 fusion.19
  (22 shorter events, 0.1 us)
Async XLA Ops:
  7.2 198.7 %copy-start = (bf16[4,128,2048]{2,1,0:T(8,128)(2,1)S(1)}, bf16[4,128,2048]{2,1,0:T(8,128)(2,1)}, u32[]{:S(2)}) copy-start(bf16[4,128,2048]{2,1,0:T(8,128)(2,1)} %param.14) | copy-start | bytes 6291460
  7.2 54.8 %all-gather.3.cloned.1.call-start = ((), (), s32[]{:S(2)}) async-start(), calls=%async_computation.5 | async-start | bytes 2359296 | tf_op jit(solution)/shard_map/all_gather | solution.py:32
  7.9 152.9 %reduce-scatter.3.cloned.1.call-start = ((), (), s32[]{:S(2)}) async-start(), calls=%async_computation.6 | async-start | bytes 9175040 | tf_op jit(solution)/shard_map/reduce_scatter | solution.py:36
  62.0 14.9 %copy-start.6 = (bf16[512,2048]{1,0:T(8,128)(2,1)S(1)}, bf16[512,2048]{1,0:T(8,128)(2,1)}, u32[]{:S(2)}) copy-start(bf16[512,2048]{1,0:T(8,128)(2,1)} %all-gather.3.cloned.1.call-done) | copy-start | bytes 6291460
  96.2 137.9 %all-gather.5.cloned.1.call-start = ((), (), s32[]{:S(2)}) async-start(), calls=%async_computation.7 | async-start | bytes 4587520 | tf_op jit(solution)/shard_map/all_gather | solution.py:39
  162.7 1.5 copy-start.4
  162.7 1.7 copy-start.3
  164.1 2.5 copy-start.5
  167.0 8.6 %copy-start.1 = (bf16[64,2048]{1,0:T(8,128)(2,1)S(1)}, bf16[64,2048]{1,0:T(8,128)(2,1)}, u32[]{:S(2)}) copy-start(bf16[64,2048]{1,0:T(8,128)(2,1)} %param.9) | copy-start | bytes 786436
  169.8 31.2 %all-to-all-start.2 = ((bf16[8,32,2048]{2,1,0:T(8,128)(2,1)}), bf16[8,32,2048]{2,1,0:T(8,128)(2,1)S(1)}, u32[]{:S(2)}, u32[]{:S(2)}) async-start(bf16[8,32,2048]{2,1,0:T(8,128)(2,1)} %bitcast.77), calls=%async_computation.4 | async-start | bytes 2097152 | tf_op jit(solution)/shard_map/all_to_all | solution.py:102
  201.0 29.8 %all-to-all-start = ((bf16[8,32,2048]{2,1,0:T(8,128)(2,1)}), bf16[8,32,2048]{2,1,0:T(8,128)(2,1)}, u32[]{:S(2)}, u32[]{:S(2)}) async-start(bf16[8,32,2048]{2,1,0:T(8,128)(2,1)} %bitcast.76), calls=%async_computation.2 | async-start | bytes 2097152 | tf_op jit(solution)/shard_map/all_to_all | solution.py:68
  205.2 58.4 %all-reduce.3.cloned.1.call-start = ((), (), s32[]{:S(2)}) async-start(), calls=%async_computation.9 | async-start | bytes 262144 | tf_op jit(solution)/shard_map/psum | solution.py:74
  233.8 114.4 %reduce-scatter.5.cloned.1.call-start = ((), (), s32[]{:S(2)}) async-start(), calls=%async_computation.8 | async-start | bytes 2359296 | tf_op jit(solution)/shard_map/reduce_scatter | solution.py:40
  264.9 6.7 %copy-start.2 = (bf16[4,8,8,128]{3,2,1,0:T(8,128)(2,1)S(1)}, bf16[4,8,8,128]{3,2,1,0:T(8,128)(2,1)}, u32[]{:S(2)}) copy-start(bf16[4,8,8,128]{3,2,1,0:T(8,128)(2,1)} %get-tuple-element.3) | copy-start | bytes 196612
  266.0 47.4 %all-to-all-start.1 = ((bf16[8,32,2048]{2,1,0:T(8,128)(2,1)}), bf16[8,32,2048]{2,1,0:T(8,128)(2,1)}, u32[]{:S(2)}, u32[]{:S(2)}) async-start(bf16[8,32,2048]{2,1,0:T(8,128)(2,1)} %bitcast.75), calls=%async_computation.3 | async-start | bytes 2097152 | tf_op jit(solution)/shard_map/all_to_all | solution.py:86
  271.5 2.2 copy-start.7
Sparse Core Ops, SparseCore 0:
  10.1 51.7 all-gather.2
  96.3 64.4 reduce-scatter.2
  164.3 31.4 all-gather.4
  233.9 29.6 all-reduce.2
  267.0 81.1 reduce-scatter.4
where the time goes:
time: 357 us
  waiting for transfers between devices  253 us (71%)
  matrix products  57.5 us (16%)
  starting transfers between devices  15.7 us (4%)
  between operations  14 us (4%)
  other arithmetic  12.2 us (3%)
  local copies, waits for them, and re-layouts  4.6 us (1%)
    reduce_scatter x1, waiting for transfers between devices, per_device(): lax.psum_scatter(partial_value.astype(jnp.bfloat16), 'tensor', scatter_di...  64.6 us
    all_gather x1, waiting for transfers between devices, per_device(): shard_rows = lax.all_gather(tokens, 'expert', axis=0, tiled=True)  54 us
    all_to_all x1, waiting for transfers between devices, per_device(): lax.all_to_all(expert_out.reshape(n_expert, per_peer, width_part), 'exper...  36.2 us
    reduce_scatter x1, waiting for transfers between devices, per_device(): lax.psum_scatter(jnp.dot(hidden_all, frozen_down_weight, preferred_elemen...  33.2 us
    all_to_all x1, waiting for transfers between devices, per_device(): lax.all_to_all(send_grads, 'expert', split_axis=0, concat_axis=0, tiled=T...  23.9 us
    all_to_all x1, waiting for transfers between devices, per_device(): lax.all_to_all(send_inputs, 'expert', split_axis=0, concat_axis=0, tiled=...  23.4 us
    psum x1, waiting for transfers between devices, per_device(): lax.psum(jnp.einsum('bcwk,cko->cbwo', incoming_input_rows, adapter_down_w...  16.4 us
    dot_general x1, matrix products, per_device(): jnp.dot(shard_rows, frozen_up_weight, preferred_element_type=jnp.float32)  14.9 us
  transfers between devices with their start and end apart: 8, of which 7 were waited for; matrix products, arithmetic and copies ran while one was open for 10% of the time, Pallas kernels for 0%

commit v1 on v0

--- a/solution.py
+++ b/solution.py
@@ -29,7 +29,15 @@
     most_slots = max(2, 4 * tok_count // all_experts)
     slot_total = all_experts * most_slots
     per_peer = expert_resident * most_slots
-    shard_rows = lax.all_gather(tokens, "expert", axis=0, tiled=True)
+    width = jax.lax.axis_size("expert")
+    y2 = [None] * width
+    kept_rows = [(p, (p + 1) % width) for p in range(width)]
+    y2[width - 1] = tokens
+    for c in range(width - 2, -1, -1):
+        y2[c] = jax.lax.ppermute(y2[c + 1], "expert", kept_rows)
+    outcome_arr = jnp.concatenate(y2, axis=0)
+    next_value = (jax.lax.axis_index("expert") + 1) * tokens.shape[0]
+    shard_rows = jnp.roll(outcome_arr, shift=next_value, axis=0)
     gate_part = jnp.dot(shard_rows, frozen_gate_weight, preferred_element_type=jnp.float32)
     up_part = jnp.dot(shard_rows, frozen_up_weight, preferred_element_type=jnp.float32)
     partial_value = jnp.concatenate([gate_part, up_part], axis=1)

time: 357 us -> 372 us (1.042)
  waiting for transfers between devices: 253 us -> 262 us
  local copies, waits for them, and re-layouts: 4.6 us -> 12.2 us
  matrix products: 57.5 us -> 52 us
    ppermute x0 -> x7, waiting for transfers between devices: none -> 66 us  [per_device(): y2[c] = jax.lax.ppermute(y2[c + 1], 'expert', kept_rows)]
    all_gather x1 -> x0, waiting for transfers between devices: 54 us -> none  [per_device(): shard_rows = lax.all_gather(tokens, 'expert', axis=0, tiled=True)]
    unnamed x18 -> x41, local copies, waits for them, and re-layouts: 0.24 us -> 6.95 us
    dot_general x1, matrix products: 14.9 us -> 9.27 us  [per_device(): jnp.dot(shard_rows, frozen_up_weight, preferred_element_type=jnp.float32)]
  transfers between devices with their start and end apart: 8 -> 14, of which waited for: 7 -> 13; matrix products, arithmetic and copies ran while one was open for 10% -> 10% of each run, Pallas kernels for 0% -> 0%
where the time goes in v1:
time: 372 us; the launch traced here: 371 us
  waiting for transfers between devices  262 us (70%)
  matrix products  52 us (14%)
  starting transfers between devices  18.6 us (5%)
  between operations  14.1 us (4%)
  local copies, waits for them, and re-layouts  12.2 us (3%)
  other arithmetic  12.2 us (3%)
    ppermute x7, waiting for transfers between devices, per_device(): y2[c] = jax.lax.ppermute(y2[c + 1], 'expert', kept_rows)  66 us
    reduce_scatter x1, waiting for transfers between devices, per_device(): lax.psum_scatter(partial_value.astype(jnp.bfloat16), 'tensor', scatter_di...  63.1 us
    all_to_all x1, waiting for transfers between devices, per_device(): lax.all_to_all(expert_out.reshape(n_expert, per_peer, width_part), 'exper...  36.2 us
    reduce_scatter x1, waiting for transfers between devices, per_device(): lax.psum_scatter(jnp.dot(hidden_all, frozen_down_weight, preferred_elemen...  33 us
    all_to_all x1, waiting for transfers between devices, per_device(): lax.all_to_all(send_grads, 'expert', split_axis=0, concat_axis=0, tiled=T...  23.9 us
    all_to_all x1, waiting for transfers between devices, per_device(): lax.all_to_all(send_inputs, 'expert', split_axis=0, concat_axis=0, tiled=...  23.2 us
    psum x1, waiting for transfers between devices, per_device(): lax.psum(jnp.einsum('bcwk,cko->cbwo', incoming_input_rows, adapter_down_w...  16.7 us
    dot_general x1, matrix products, per_device(): jnp.dot(hidden_all, frozen_down_weight, preferred_element_type=jnp.float32)  13.1 us
  transfers between devices with their start and end apart: 14, of which 13 were waited for; matrix products, arithmetic and copies ran while one was open for 10% of the time, Pallas kernels for 0%

profile of v1, /device:TPU:0, one launch (start us, length us, event | category | flops | bytes accessed | tf_op | source)
XLA Modules:
  0.0 371.4 jit_solution(1128613157754428396)
XLA Ops:
  7.2 3.0 collective-permute-start
  10.3 9.6 %collective-permute-done = bf16[64,2048]{1,0:T(8,128)(2,1)S(1)} collective-permute-done((bf16[64,2048]{1,0:T(8,128)(2,1)}, bf16[64,2048]{1,0:T(8,128)(2,1)S(1)}, u32[]{:S(2)}, u32[]{:S(2)}) %collective-permute-start) | collective-permute-done | bytes 262176 | tf_op jit(solution)/shard_map/ppermute | solution.py:37
  19.8 10.2 %collective-permute-done.1 = bf16[64,2048]{1,0:T(8,128)(2,1)S(1)} collective-permute-done((bf16[64,2048]{1,0:T(8,128)(2,1)S(1)}, bf16[64,2048]{1,0:T(8,128)(2,1)S(1)}, u32[]{:S(2)}, u32[]{:S(2)}) %collective-permute-start.1) | collective-permute-done | bytes 262176 | tf_op jit(solution)/shard_map/ppermute | solution.py:37
  30.0 9.3 %collective-permute-done.2 = bf16[64,2048]{1,0:T(8,128)(2,1)S(1)} collective-permute-done((bf16[64,2048]{1,0:T(8,128)(2,1)S(1)}, bf16[64,2048]{1,0:T(8,128)(2,1)S(1)}, u32[]{:S(2)}, u32[]{:S(2)}) %collective-permute-start.2) | collective-permute-done | bytes 262176 | tf_op jit(solution)/shard_map/ppermute | solution.py:37
  39.3 9.1 %collective-permute-done.3 = bf16[64,2048]{1,0:T(8,128)(2,1)S(1)} collective-permute-done((bf16[64,2048]{1,0:T(8,128)(2,1)S(1)}, bf16[64,2048]{1,0:T(8,128)(2,1)S(1)}, u32[]{:S(2)}, u32[]{:S(2)}) %collective-permute-start.3) | collective-permute-done | bytes 262176 | tf_op jit(solution)/shard_map/ppermute | solution.py:37
  48.4 9.1 %collective-permute-done.4 = bf16[64,2048]{1,0:T(8,128)(2,1)S(1)} collective-permute-done((bf16[64,2048]{1,0:T(8,128)(2,1)S(1)}, bf16[64,2048]{1,0:T(8,128)(2,1)S(1)}, u32[]{:S(2)}, u32[]{:S(2)}) %collective-permute-start.4) | collective-permute-done | bytes 262176 | tf_op jit(solution)/shard_map/ppermute | solution.py:37
  57.4 0.7 copy-done.2
  58.1 9.5 %collective-permute-done.5 = bf16[64,2048]{1,0:T(8,128)(2,1)} collective-permute-done((bf16[64,2048]{1,0:T(8,128)(2,1)S(1)}, bf16[64,2048]{1,0:T(8,128)(2,1)}, u32[]{:S(2)}, u32[]{:S(2)}) %collective-permute-start.5) | collective-permute-done | bytes 262176 | tf_op jit(solution)/shard_map/ppermute | solution.py:37
  67.6 9.4 %collective-permute-done.6 = bf16[64,2048]{1,0:T(8,128)(2,1)} collective-permute-done((bf16[64,2048]{1,0:T(8,128)(2,1)}, bf16[64,2048]{1,0:T(8,128)(2,1)}, u32[]{:S(2)}, u32[]{:S(2)}) %collective-permute-start.6) | collective-permute-done | bytes 262176 | tf_op jit(solution)/shard_map/ppermute | solution.py:37
  77.0 1.0 constant_dynamic-update-slice_fusion.15
  78.0 1.0 constant_dynamic-update-slice_fusion.14
  78.9 1.0 constant_dynamic-update-slice_fusion.13
  80.0 1.0 constant_dynamic-update-slice_fusion.8
  81.0 1.0 constant_dynamic-update-slice_fusion.7
  82.0 1.0 constant_dynamic-update-slice_fusion.6
  83.2 12.5 %convolution_convert_fusion.1 = bf16[512,3584]{1,0:T(8,128)(2,1)} fusion(bf16[2048,3584]{1,0:T(8,128)(2,1)} %param.10, bf16[1024,2048]{1,0:T(8,128)(2,1)S(1)} %constant_dynamic-update-slice_fusion, s32[]{:T(128)S(6)} %select_n.14), kind=kOutput, calls=%fused_computation.2 | convolution fusion | flops 7518027776 | bytes 20447236 | tf_op jit(solution)/shard_map/dot_general | solution.py:41
  95.7 9.3 %convolution_convert_fusion = bf16[512,3584]{1,0:T(8,128)(2,1)} fusion(bf16[2048,3584]{1,0:T(8,128)(2,1)S(1)} %bitcast.77, bf16[1024,2048]{1,0:T(8,128)(2,1)S(1)} %constant_dynamic-update-slice_fusion, s32[]{:T(128)S(6)} %select_n.14), kind=kOutput, calls=%fused_computation.1 | convolution fusion | flops 7518027776 | bytes 20447236 | tf_op jit(solution)/shard_map/dot_general | solution.py:42
  104.9 6.9 %pad_maximum_fusion = bf16[512,7168]{1,0:T(8,128)(2,1)} fusion(bf16[512,3584]{1,0:T(8,128)(2,1)} %convolution_convert_fusion, bf16[512,3584]{1,0:T(8,128)(2,1)} %convolution_convert_fusion.1), kind=kLoop, calls=%fused_computation | loop fusion | flops 14680064 | bytes 14680064 | tf_op jit(solution)/shard_map/concatenate | solution.py:43
  111.9 63.1 %reduce-scatter.3.cloned.1.call-done = bf16[128,7168]{1,0:T(8,128)(2,1)} async-done(((bf16[512,7168]{1,0:T(8,128)(2,1)}), bf16[128,7168]{1,0:T(8,128)(2,1)}) %reduce-scatter.3.cloned.1.call-update) | async-done | bytes 1835024 | tf_op jit(solution)/shard_map/reduce_scatter | solution.py:44
  175.0 1.9 convert_element_type.72
  176.9 1.4 fusion.8
  178.5 0.1 reshape.81
  178.6 1.5 mul.82
  180.1 1.7 mul.83
  181.9 0.1 mul.80
  182.0 0.2 fusion.15
  182.2 2.7 convolution_convert_fusion.3
  184.9 5.5 %all-to-all-start.2 = ((bf16[8,32,2048]{2,1,0:T(8,128)(2,1)}), bf16[8,32,2048]{2,1,0:T(8,128)(2,1)S(1)}, u32[]{:S(2)}, u32[]{:S(2)}) async-start(bf16[8,32,2048]{2,1,0:T(8,128)(2,1)} %bitcast.75), calls=%async_computation.4 | async-start | bytes 2097152 | tf_op jit(solution)/shard_map/all_to_all | solution.py:110
  190.4 0.1 convert_element_type.79
  190.7 1.4 convolution_convert_fusion.5
  192.2 23.9 %all-to-all-done.2 = bf16[8,32,2048]{2,1,0:T(8,128)(2,1)S(1)} async-done(((bf16[8,32,2048]{2,1,0:T(8,128)(2,1)}), bf16[8,32,2048]{2,1,0:T(8,128)(2,1)S(1)}, u32[]{:S(2)}, u32[]{:S(2)}) %all-to-all-start.2) | async-done | bytes 1048608 | tf_op jit(solution)/shard_map/all_to_all | solution.py:110
  216.1 4.2 %all-to-all-start = ((bf16[8,32,2048]{2,1,0:T(8,128)(2,1)}), bf16[8,32,2048]{2,1,0:T(8,128)(2,1)}, u32[]{:S(2)}, u32[]{:S(2)}) async-start(bf16[8,32,2048]{2,1,0:T(8,128)(2,1)} %bitcast.74), calls=%async_computation.2 | async-start | bytes 2097152 | tf_op jit(solution)/shard_map/all_to_all | solution.py:76
  220.3 0.2 all-reduce.3.cloned.1.call-start
  220.5 0.6 copy.46
  221.1 1.5 fusion.9
  222.6 23.2 %all-to-all-done = bf16[8,32,2048]{2,1,0:T(8,128)(2,1)} async-done(((bf16[8,32,2048]{2,1,0:T(8,128)(2,1)}), bf16[8,32,2048]{2,1,0:T(8,128)(2,1)}, u32[]{:S(2)}, u32[]{:S(2)}) %all-to-all-start) | async-done | bytes 1048608 | tf_op jit(solution)/shard_map/all_to_all | solution.py:76
  245.8 3.0 fusion.12
  249.0 13.1 %convolution_convert_fusion.2 = bf16[512,2048]{1,0:T(8,128)(2,1)} fusion(bf16[512,3584]{1,0:T(8,128)(2,1)} %all-gather.2.cloned.1.call-done, bf16[3584,2048]{1,0:T(8,128)(2,1)} %param.12), kind=kOutput, calls=%fused_computation.5 | convolution fusion | flops 7517241344 | bytes 20447232 | tf_op jit(solution)/shard_map/dot_general | solution.py:49
  262.1 16.7 %all-reduce.3.cloned.1.call-done = (bf16[4,8,8,128]{3,2,1,0:T(8,128)(2,1)}, bf16[4,8,8,128]{3,1,2,0:T(8,128)(2,1)}) async-done(((bf16[4,8,8,128]{3,2,1,0:T(8,128)(2,1)}, bf16[4,8,8,128]{3,1,2,0:T(8,128)(2,1)}), (bf16[4,8,8,128]{3,2,1,0:T(8,128)(2,1)}, bf16[4,8,8,128]{3,1,2,0:T(8,128)(2,1)})) %all-reduce.3.cloned.1.call-update) | async-done | bytes 131088 | tf_op jit(solution)/shard_map/psum | solution.py:82
  278.7 1.3 fusion
  280.1 1.0 copy.62
  281.1 5.5 %all-to-all-start.1 = ((bf16[8,32,2048]{2,1,0:T(8,128)(2,1)}), bf16[8,32,2048]{2,1,0:T(8,128)(2,1)}, u32[]{:S(2)}, u32[]{:S(2)}) async-start(bf16[8,32,2048]{2,1,0:T(8,128)(2,1)} %bitcast.73), calls=%async_computation.3 | async-start | bytes 2097152 | tf_op jit(solution)/shard_map/all_to_all | solution.py:94
  286.8 2.1 bitcast_convert_fusion
  288.8 3.5 bitcast_convert_fusion.1
  292.3 36.2 %all-to-all-done.1 = bf16[8,32,2048]{2,1,0:T(8,128)(2,1)} async-done(((bf16[8,32,2048]{2,1,0:T(8,128)(2,1)}), bf16[8,32,2048]{2,1,0:T(8,128)(2,1)}, u32[]{:S(2)}, u32[]{:S(2)}) %all-to-all-start.1) | async-done | bytes 1048608 | tf_op jit(solution)/shard_map/all_to_all | solution.py:94
  328.5 1.5 fusion.25
  330.0 33.0 %reduce-scatter.5.cloned.1.call-done = bf16[64,2048]{1,0:T(8,128)(2,1)} async-done(((bf16[512,2048]{1,0:T(8,128)(2,1)}), bf16[64,2048]{1,0:T(8,128)(2,1)}) %reduce-scatter.5.cloned.1.call-update) | async-done | bytes 262160 | tf_op jit(solution)/shard_map/reduce_scatter | solution.py:48
  363.1 1.8 fusion.21
  (58 shorter events, 1.0 us)
Async XLA Ops:
  7.2 214.0 %copy-start = (bf16[4,128,2048]{2,1,0:T(8,128)(2,1)S(1)}, bf16[4,128,2048]{2,1,0:T(8,128)(2,1)}, u32[]{:S(2)}) copy-start(bf16[4,128,2048]{2,1,0:T(8,128)(2,1)} %param.14) | copy-start | bytes 6291460
  7.2 75.9 %copy-start.1 = (bf16[64,2048]{1,0:T(8,128)(2,1)S(1)}, bf16[64,2048]{1,0:T(8,128)(2,1)}, u32[]{:S(2)}) copy-start(bf16[64,2048]{1,0:T(8,128)(2,1)} %param.9) | copy-start | bytes 786436
  7.2 167.8 %reduce-scatter.3.cloned.1.call-start = ((), (), s32[]{:S(2)}) async-start(), calls=%async_computation.5 | async-start | bytes 9175040 | tf_op jit(solution)/shard_map/reduce_scatter | solution.py:44
  7.2 12.6 %collective-permute-start = (bf16[64,2048]{1,0:T(8,128)(2,1)}, bf16[64,2048]{1,0:T(8,128)(2,1)S(1)}, u32[]{:S(2)}, u32[]{:S(2)}) collective-permute-start(bf16[64,2048]{1,0:T(8,128)(2,1)} %param.9), channel_id=1, source_target_pairs={{0,4},{4,8},{8,12},{12,16},{16,20},{20,24},{24,28},{28,0},{1,5},{5... | collective-permute-start | bytes 786440 | tf_op jit(solution)/shard_map/ppermute | solution.py:37
  19.8 10.2 %collective-permute-start.1 = (bf16[64,2048]{1,0:T(8,128)(2,1)S(1)}, bf16[64,2048]{1,0:T(8,128)(2,1)S(1)}, u32[]{:S(2)}, u32[]{:S(2)}) collective-permute-start(bf16[64,2048]{1,0:T(8,128)(2,1)S(1)} %collective-permute-done), channel_id=1, source_target_pairs={{0,4},{4,8},{8,12},{12,16},{16,20},{20,24},{24,28},{28,0},{1,5},{5... | collective-permute-start | bytes 786440 | tf_op jit(solution)/shard_map/ppermute | solution.py:37
  30.0 9.3 %collective-permute-start.2 = (bf16[64,2048]{1,0:T(8,128)(2,1)S(1)}, bf16[64,2048]{1,0:T(8,128)(2,1)S(1)}, u32[]{:S(2)}, u32[]{:S(2)}) collective-permute-start(bf16[64,2048]{1,0:T(8,128)(2,1)S(1)} %collective-permute-done.1), channel_id=1, source_target_pairs={{0,4},{4,8},{8,12},{12,16},{16,20},{20,24},{24,28},{28,0},{1,5},{5... | collective-permute-start | bytes 786440 | tf_op jit(solution)/shard_map/ppermute | solution.py:37
  39.3 9.1 %collective-permute-start.3 = (bf16[64,2048]{1,0:T(8,128)(2,1)S(1)}, bf16[64,2048]{1,0:T(8,128)(2,1)S(1)}, u32[]{:S(2)}, u32[]{:S(2)}) collective-permute-start(bf16[64,2048]{1,0:T(8,128)(2,1)S(1)} %collective-permute-done.2), channel_id=1, source_target_pairs={{0,4},{4,8},{8,12},{12,16},{16,20},{20,24},{24,28},{28,0},{1,5},{5... | collective-permute-start | bytes 786440 | tf_op jit(solution)/shard_map/ppermute | solution.py:37
  48.4 9.1 %collective-permute-start.4 = (bf16[64,2048]{1,0:T(8,128)(2,1)S(1)}, bf16[64,2048]{1,0:T(8,128)(2,1)S(1)}, u32[]{:S(2)}, u32[]{:S(2)}) collective-permute-start(bf16[64,2048]{1,0:T(8,128)(2,1)S(1)} %collective-permute-done.3), channel_id=1, source_target_pairs={{0,4},{4,8},{8,12},{12,16},{16,20},{20,24},{24,28},{28,0},{1,5},{5... | collective-permute-start | bytes 786440 | tf_op jit(solution)/shard_map/ppermute | solution.py:37
  57.4 0.7 copy-start.2
  58.1 9.5 %collective-permute-start.5 = (bf16[64,2048]{1,0:T(8,128)(2,1)S(1)}, bf16[64,2048]{1,0:T(8,128)(2,1)}, u32[]{:S(2)}, u32[]{:S(2)}) collective-permute-start(bf16[64,2048]{1,0:T(8,128)(2,1)S(1)} %collective-permute-done.4), channel_id=1, source_target_pairs={{0,4},{4,8},{8,12},{12,16},{16,20},{20,24},{24,28},{28,0},{1,5},{5... | collective-permute-start | bytes 786440 | tf_op jit(solution)/shard_map/ppermute | solution.py:37
  67.6 9.4 %collective-permute-start.6 = (bf16[64,2048]{1,0:T(8,128)(2,1)}, bf16[64,2048]{1,0:T(8,128)(2,1)}, u32[]{:S(2)}, u32[]{:S(2)}) collective-permute-start(bf16[64,2048]{1,0:T(8,128)(2,1)} %collective-permute-done.5), channel_id=1, source_target_pairs={{0,4},{4,8},{8,12},{12,16},{16,20},{20,24},{24,28},{28,0},{1,5},{5... | collective-permute-start | bytes 786440 | tf_op jit(solution)/shard_map/ppermute | solution.py:37
  67.6 15.3 %copy-start.3 = (bf16[64,2048]{1,0:T(8,128)(2,1)S(1)}, bf16[64,2048]{1,0:T(8,128)(2,1)}, u32[]{:S(2)}) copy-start(bf16[64,2048]{1,0:T(8,128)(2,1)} %copy-done.2) | copy-start | bytes 786436
  83.0 12.6 %slice-start = ((s8[14680064]{0:T(1024)(128)(4,1)}), s8[4194304]{0:T(1024)(128)(4,1)S(1)}, s32[]{:S(2)}) async-start(s8[14680064]{0:T(1024)(128)(4,1)} %bitcast.76), calls=%async_computation.9 | async-start | bytes 8388608
  83.1 12.5 %slice-start.1 = ((s8[14680064]{0:T(1024)(128)(4,1)}), s8[4194304]{0:T(1024)(128)(4,1)S(1)}, s32[]{:S(2)}) async-start(s8[14680064]{0:T(1024)(128)(4,1)} %bitcast.76), calls=%async_computation.10 | async-start | bytes 8388608
  83.1 12.5 %slice-start.2 = ((s8[14680064]{0:T(1024)(128)(4,1)}), s8[4194304]{0:T(1024)(128)(4,1)S(1)}, s32[]{:S(2)}) async-start(s8[14680064]{0:T(1024)(128)(4,1)} %bitcast.76), calls=%async_computation.11 | async-start | bytes 8388608
  83.2 12.5 %slice-start.3 = ((s8[14680064]{0:T(1024)(128)(4,1)}), s8[2097152]{0:T(1024)(128)(4,1)S(1)}, s32[]{:S(2)}) async-start(s8[14680064]{0:T(1024)(128)(4,1)} %bitcast.76), calls=%async_computation.12 | async-start | bytes 4194304
  111.8 66.5 %copy-start.5 = (s32[64,2]{0,1:T(2,128)S(1)}, s32[64,2]{0,1:T(2,128)}, u32[]{:S(2)}) copy-start(s32[64,2]{0,1:T(2,128)} %param.15) | copy-start | bytes 1540
  111.8 137.1 %all-gather.2.cloned.1.call-start = ((), (), s32[]{:S(2)}) async-start(), calls=%async_computation.6 | async-start | bytes 4587520 | tf_op jit(solution)/shard_map/all_gather | solution.py:47
  176.9 4.9 %copy-start.6 = (f32[64,2]{0,1:T(2,128)S(1)}, f32[64,2]{0,1:T(2,128)}, u32[]{:S(2)}) copy-start(f32[64,2]{0,1:T(2,128)} %param.16) | copy-start | bytes 1540
  184.9 31.2 %all-to-all-start.2 = ((bf16[8,32,2048]{2,1,0:T(8,128)(2,1)}), bf16[8,32,2048]{2,1,0:T(8,128)(2,1)S(1)}, u32[]{:S(2)}, u32[]{:S(2)}) async-start(bf16[8,32,2048]{2,1,0:T(8,128)(2,1)} %bitcast.75), calls=%async_computation.4 | async-start | bytes 2097152 | tf_op jit(solution)/shard_map/all_to_all | solution.py:110
  216.1 29.8 %all-to-all-start = ((bf16[8,32,2048]{2,1,0:T(8,128)(2,1)}), bf16[8,32,2048]{2,1,0:T(8,128)(2,1)}, u32[]{:S(2)}, u32[]{:S(2)}) async-start(bf16[8,32,2048]{2,1,0:T(8,128)(2,1)} %bitcast.74), calls=%async_computation.2 | async-start | bytes 2097152 | tf_op jit(solution)/shard_map/all_to_all | solution.py:76
  220.3 58.4 %all-reduce.3.cloned.1.call-start = ((), (), s32[]{:S(2)}) async-start(), calls=%async_computation.8 | async-start | bytes 262144 | tf_op jit(solution)/shard_map/psum | solution.py:82
  248.9 114.2 %reduce-scatter.5.cloned.1.call-start = ((), (), s32[]{:S(2)}) async-start(), calls=%async_computation.7 | async-start | bytes 2359296 | tf_op jit(solution)/shard_map/reduce_scatter | solution.py:48
  278.7 8.0 %copy-start.4 = (bf16[4,8,8,128]{3,2,1,0:T(8,128)(2,1)S(1)}, bf16[4,8,8,128]{3,2,1,0:T(8,128)(2,1)}, u32[]{:S(2)}) copy-start(bf16[4,8,8,128]{3,2,1,0:T(8,128)(2,1)} %get-tuple-element.3) | copy-start | bytes 196612
  280.1 8.8 %copy-start.7 = (bf16[4,8,8,128]{3,1,2,0:T(8,128)(2,1)S(1)}, bf16[4,8,8,128]{3,1,2,0:T(8,128)(2,1)}, u32[]{:S(2)}) copy-start(bf16[4,8,8,128]{3,1,2,0:T(8,128)(2,1)} %get-tuple-element.4) | copy-start | bytes 196612
  281.1 47.4 %all-to-all-start.1 = ((bf16[8,32,2048]{2,1,0:T(8,128)(2,1)}), bf16[8,32,2048]{2,1,0:T(8,128)(2,1)}, u32[]{:S(2)}, u32[]{:S(2)}) async-start(bf16[8,32,2048]{2,1,0:T(8,128)(2,1)} %bitcast.73), calls=%async_computation.3 | async-start | bytes 2097152 | tf_op jit(solution)/shard_map/all_to_all | solution.py:94
Sparse Core Ops, SparseCore 0:
  111.9 63.0 reduce-scatter.2
  178.5 31.4 all-gather.1
  249.0 29.6 all-reduce.2
  282.1 80.9 reduce-scatter.4
